TPU v7x, 256 devices: a whole 4x4x8 slice. The times are simulated.
256 devices in a mesh: dom: 32 (over z, x), head: 8 (over y, core).
Axes of the slice: x: 4, y: 4, z: 8, core: 2. Of those that a mesh axis runs over, the one named last changes fastest.
Arguments:
- node_feats: float32 [32768, 512], P('dom')
- order: int32 [32768], P('dom'), may hold values from 0 to 32767, as said below
- node_count: int32 [256], replicated, may hold values from 32 to 128
- local_blocks: int32 [256, 3], P('dom'), may hold values from 0 to 255, as said below
- exp_blocks: int32 [256, 6], P('dom'), may hold values from 0 to 255, as said below
- virt_blocks: int32 [256], P('dom'), may hold values from 0 to 3
- virt_feats: float32 [512, 512], replicated, may hold values from -6 to 6
- w_query: float32 [512, 512], P(None, 'head'), may hold values from -0.25 to 0.25
- w_key: float32 [512, 512], P(None, 'head'), may hold values from -0.25 to 0.25
- w_value: float32 [512, 512], P(None, 'head'), may hold values from -0.25 to 0.25
- w_out: float32 [512, 512], P(None, 'head'), may hold values from -2 to 2
- w_up: float32 [512, 1024], P(None, 'head'), may hold values from -0.25 to 0.25
- w_down: float32 [1024, 512], P('head'), may hold values from -0.1875 to 0.1875
Outputs:
- refined: float32 [32768, 512], P('dom', 'head')
Inputs may be any that keep to these rules, and one draw needn't show every extreme that they name: `order`: each device's 8 * 128 entries are a permutation of that device's own node numbers (the rows it holds). `local_blocks`: every entry lies within 2 clusters of its own cluster; column 1 is exactly 2 away unless that leaves the grid, where it is clipped to the end. `exp_blocks`: call id // 8 the owner of a cluster id. Among the 48 entries of one device's clusters, at most 3 have any one owner, and for every device some owner has exactly 3.
All inputs are finite; a program needn't handle non-finite values.
Results may differ from a plain program's by a relative error of at most 0.0003.
Values sent between devices are 32-bit elements; how exact they have to be, the bound alone decides.
No kernel may reach another device: no remote copies, remote signals or barrier semaphores. Data moves between devices by JAX's collectives and lax.ppermute only.
A program may use at most 128 MiB of HBM per device.

v0:
```python
import math
import jax
import jax.numpy as jnp
from jax import lax
from jax.sharding import PartitionSpec as P

D = 512
HD = 64
NE = 6
LW = 2
highest = lax.Precision.HIGHEST


def with_halo(value, sides, width):
    for axis, dim in sides:
        size, length = (lax.axis_size(axis), value.shape[dim])
        up = [(i, (i + 1) % size) for i in range(size - 1)]
        down = [(j, i) for i, j in up]
        last = lax.slice_in_dim(value, length - width, length, axis=dim)
        initial = lax.slice_in_dim(value, 0, width, axis=dim)
        before = lax.ppermute(last, axis, up)
        after = lax.ppermute(initial, axis, down)
        value = jnp.concatenate([before, value, after], axis=dim)
    return value


def matmul(left, right):
    return jnp.dot(left, right, preferred_element_type=jnp.float32, precision=highest)


def partial_softmax(queries, keyvals, usable, head_width):
    batch_size = queries.shape[0]
    head_count = queries.shape[2]
    head_size = queries.shape[3]
    key_rows = keyvals[..., :head_width].reshape(batch_size, -1, head_count, head_size)
    value_rows = keyvals[..., head_width:].reshape(batch_size, -1, head_count, head_size)
    scores = jnp.einsum("bqhd,bkhd->bhqk", queries, key_rows, precision=highest) / math.sqrt(
        head_size
    )
    scores = jnp.where(usable[:, None, None, :], scores, -1e30)
    peaks = jnp.max(scores, axis=3)
    weights = jnp.where(usable[:, None, None, :], jnp.exp(scores - peaks[..., None]), 0.0)
    totals = jnp.sum(weights, axis=3)
    weighted = jnp.einsum("bhqk,bkhd->bqhd", weights, value_rows, precision=highest)
    return (peaks, totals, weighted)


def shards(
    node_feats,
    order,
    node_count,
    local_blocks,
    exp_blocks,
    virt_blocks,
    virt_feats,
    w_query,
    w_key,
    w_value,
    w_out,
    w_up,
    w_down,
):
    dom_size = lax.axis_size("dom")
    clus_dev = local_blocks.shape[0]
    rows_dev = node_feats.shape[0]
    clus_rows = rows_dev // clus_dev
    head_width = w_query.shape[1]
    head_count = head_width // HD
    capacity = max(2, 5 * clus_dev * NE // (2 * dom_size))
    base_row = lax.axis_index("dom") * rows_dev
    first_cluster = lax.axis_index("dom") * clus_dev
    local_order = order - base_row
    ordered = jnp.take(node_feats, local_order, axis=0)
    queries = matmul(ordered, w_query).reshape(clus_dev, clus_rows, head_count, HD)
    keyvals = jnp.concatenate([matmul(ordered, w_key), matmul(ordered, w_value)], 1).reshape(
        clus_dev, clus_rows, 2 * head_width
    )
    virt_kv = jnp.concatenate([matmul(virt_feats, w_key), matmul(virt_feats, w_value)], 1).reshape(
        -1, clus_rows, 2 * head_width
    )
    virt_near = jnp.take(virt_kv, virt_blocks, axis=0)
    positions = jnp.arange(clus_rows)

    def row_usable(block_ids):
        return positions < jnp.take(node_count, block_ids)[..., None]

    padded = with_halo(keyvals, (("dom", 0),), LW)
    near_kv = jnp.take(padded, local_blocks - (first_cluster - LW), axis=0)
    near_usable = row_usable(local_blocks)
    virt_usable = jnp.ones((clus_dev, 1, clus_rows), bool)
    far_usable = row_usable(exp_blocks)
    flat_ids = exp_blocks.reshape(-1)
    owners = flat_ids // clus_dev
    inside = flat_ids % clus_dev
    onehot = (owners[:, None] == jnp.arange(dom_size)[None, :]).astype(jnp.int32)
    slots = jnp.sum((jnp.cumsum(onehot, 0) - onehot) * onehot, 1)
    request = jnp.zeros((dom_size, capacity), jnp.int32).at[owners, slots].set(inside)
    blocks = jnp.take(
        keyvals, lax.all_to_all(request, "dom", split_axis=0, concat_axis=0, tiled=True), axis=0
    )
    arrived = lax.all_to_all(blocks, "dom", split_axis=0, concat_axis=0, tiled=True)
    far_kv = arrived[owners, slots].reshape(clus_dev, NE, clus_rows, 2 * head_width)
    every_kv = jnp.concatenate([near_kv, far_kv, virt_near[:, None]], 1).reshape(
        clus_dev, -1, 2 * head_width
    )
    every_usable = jnp.concatenate([near_usable, far_usable, virt_usable], 1).reshape(clus_dev, -1)
    peaks, totals, weighted = partial_softmax(queries, every_kv, every_usable, head_width)
    attention = weighted / jnp.transpose(totals, (0, 2, 1))[..., None]
    heads_flat = attention.reshape(rows_dev, head_width)
    col_width = w_out.shape[1]
    projected = matmul(lax.all_gather(heads_flat, "head", axis=1, tiled=True), w_out)
    col_start = lax.axis_index("head") * col_width
    residual = lax.dynamic_slice_in_dim(ordered, col_start, col_width, 1) + projected
    row_sums, row_squares = lax.psum(
        (jnp.sum(residual, 1), jnp.sum(residual * residual, 1)), "head"
    )
    row_mean = row_sums / D
    row_var = row_squares / D - row_mean * row_mean
    normed = (residual - row_mean[:, None]) * lax.rsqrt(row_var + 1e-05)[:, None]
    hidden = matmul(lax.all_gather(normed, "head", axis=1, tiled=True), w_up)
    activated = jax.nn.gelu(hidden, approximate=False)
    partials = matmul(activated, w_down)
    feed_forward = lax.psum_scatter(partials, "head", scatter_dimension=1, tiled=True)
    result = residual + feed_forward
    return jnp.zeros_like(result).at[local_order].set(result)


def solution(mesh):
    return jax.shard_map(
        shards,
        mesh=mesh,
        in_specs=(
            P("dom", None),
            P("dom"),
            P(),
            P("dom", None),
            P("dom", None),
            P("dom"),
            P(),
            P(None, "head"),
            P(None, "head"),
            P(None, "head"),
            P(None, "head"),
            P(None, "head"),
            P("head", None),
        ),
        out_specs=P("dom", "head"),
        check_vma=False,
    )
```

profile of v0, /device:TPU:2, one launch (start us, length us, event | category | flops | bytes accessed | tf_op | source)
XLA Modules:
  0.0 362.6 jit_solution(8832196854405304521)
XLA Ops:
  8.6 2.8 scatter_fusion
  12.1 11.6 %all-to-all-start = ((s32[32,1,3]{2,1,0:T(1,128)}), s32[32,1,3]{2,1,0:T(1,128)S(1)}, u32[]{:S(2)}, u32[]{:S(2)}) async-start(s32[32,1,3]{2,1,0:T(1,128)} %copy.52), calls=%async_computation | async-start | bytes 32768 | tf_op jit(solution)/shard_map/all_to_all | solution.py:99
  24.4 4.9 %gather_fusion = f32[1024,512]{1,0:T(8,128)} fusion(f32[1024,512]{1,0:T(8,128)S(1)} %copy-done, s32[1024]{0:T(1024)S(1)} %broadcast_clamp_fusion), kind=kCustom, calls=%fused_computation | custom fusion | bytes 4198400 | tf_op jit(solution)/shard_map/jit(_take)/gather | solution.py:73
  29.3 2.9 copy.47
  32.2 1.8 broadcast_select_fusion.1
  34.0 1.5 fusion.153
  35.5 1.5 fusion.152
  39.6 3.6 gather_fusion.2
  43.2 5.9 %broadcast_select_fusion = f32[32,3,128,128]{3,2,1,0:T(8,128)} fusion(f32[32,3,128,128]{3,2,1,0:T(8,128)} %bitcast.82, pred[32,3]{1,0:T(8,128)(4,1)S(1)} %copy.54), kind=kLoop, calls=%fused_computation.17 | loop fusion | flops 1572864 | bytes 12583008 | tf_op jit(solution)/shard_map/jit(_take)/select_n | solution.py:98
  49.1 9.8 %all-to-all-start.1 = ((f32[32,3,128,128]{3,2,1,0:T(8,128)}), f32[32,3,128,128]{3,2,1,0:T(8,128)}, u32[]{:S(2)}, u32[]{:S(2)}) async-start(f32[32,3,128,128]{3,2,1,0:T(8,128)} %broadcast_select_fusion), calls=%async_computation.1 | async-start | bytes 12582912 | tf_op jit(solution)/shard_map/all_to_all | solution.py:101
  59.7 1.7 copy.72
  61.3 2.2 collective-permute-start.1
  64.3 4.1 %collective-permute-start = (f32[2,128,128]{2,1,0:T(8,128)}, f32[2,128,128]{2,1,0:T(8,128)}, u32[]{:S(2)}, u32[]{:S(2)}) collective-permute-start(f32[2,128,128]{2,1,0:T(8,128)} %bitcast), channel_id=1, source_target_pairs={{0,8},{8,16},{16,24},{24,32},{32,40},{40,48},{48,56},{56,64},{64,7... | collective-permute-start | bytes 393224 | tf_op jit(solution)/shard_map/ppermute | solution.py:21
  68.4 2.4 fusion.155
  70.7 2.4 fusion.154
  77.9 3.7 %convolution_bitcast_fusion = f32[8,8,8,128]{3,2,1,0:T(8,128)} fusion(f32[1024,512]{0,1:T(8,128)} %copy-done.2, f32[512,64]{0,1:T(8,128)} %param.20), kind=kOutput, calls=%fused_computation.22 | convolution fusion | flops 402653184 | bytes 2490368 | tf_op jit(solution)/shard_map/dot_general | solution.py:28
  81.7 3.4 collective-permute-done.1
  86.2 1.8 gather_fusion.1
  88.0 2.8 broadcast_select_fusion.2
  90.7 106.3 %all-to-all-done.1 = f32[32,3,128,128]{3,2,1,0:T(8,128)} async-done(((f32[32,3,128,128]{3,2,1,0:T(8,128)}), f32[32,3,128,128]{3,2,1,0:T(8,128)}, u32[]{:S(2)}, u32[]{:S(2)}) %all-to-all-start.1) | async-done | bytes 6291488 | tf_op jit(solution)/shard_map/all_to_all | solution.py:101
  197.0 5.4 %gather_fusion.3 = f32[48,128,128]{2,1,0:T(8,128)} fusion(f32[32,3,128,128]{3,2,1,0:T(8,128)} %all-to-all-done.1, s32[48]{0:T(128)S(1)} %get-tuple-element.11), kind=kCustom, calls=%fused_computation.3 | custom fusion | bytes 6291840 | tf_op jit(solution)/shard_map/gather | solution.py:102
  202.5 2.8 pad_maximum_fusion
  205.3 6.1 %fusion.151 = (f32[8,128]{1,0:T(8,128)S(1)}, f32[8,128,1280]{2,1,0:T(8,128)S(1)}) fusion(f32[8,1280,128]{2,1,0:T(8,128)S(1)} %bitcast.80, f32[8,8,8,128]{3,2,1,0:T(8,128)S(1)} %copy-done.4, pred[8,1280]{1,0:T(8,128)(4,1)S(1)} %add_bitcast_fusion), kind=kOutput, calls=%fused_computation.216 | convolution fusion | flops 1010564096 | bytes 10762240 | tf_op jit(solution)/shard_map/bqhd,bkhd->bhqk/dot_general | solution.py:37
  212.5 10.5 %fusion.16 = f32[8,128,1,64]{1,3,0,2:T(8,128)S(1)} fusion(f32[8,128,1280]{2,1,0:T(8,128)S(1)} %get-tuple-element.22, f32[8,128]{1,0:T(8,128)S(1)} %get-tuple-element.21, pred[8,1280]{1,0:T(8,128)(4,1)S(1)} %add_bitcast_fusion, f32[8,1280,128]{2,1,0:T(8,128)S(1)} %bitcast.81, f32[8,128]{1,0:T(8,128)S(1)} %fusion.6), kind=kOutput, calls=%fused_computation.25 | convolution fusion | flops 1009319936 | bytes 10766336 | tf_op jit(solution)/shard_map/bhqk,bkhd->bqhd/dot_general | solution.py:44
  224.0 35.8 %all-gather.3.cloned.1.call-done = f32[1024,512]{0,1:T(8,128)} async-done(((f32[1024,64]{0,1:T(8,128)}), f32[1024,512]{0,1:T(8,128)}) %all-gather.3.cloned.1.call-update) | async-done | bytes 2097168 | tf_op jit(solution)/shard_map/all_gather | solution.py:111
  259.8 3.0 fusion.150
  262.9 14.2 %all-reduce = (f32[1024]{0:T(1024)S(1)}, f32[1024]{0:T(1024)S(1)}) all-reduce(f32[1024]{0:T(1024)S(1)} %get-tuple-element.6, f32[1024]{0:T(1024)S(1)} %get-tuple-element.5), channel_id=1, replica_groups=mesh['dom'=32,'head'=8] {'head'}, use_global_device_ids=true, to_apply=%region_8.9 | all-reduce | flops 2048 | bytes 16384 | tf_op jit(solution)/shard_map/psum | solution.py:114
  278.1 26.5 %all-gather.5.cloned.1.call-done = f32[1024,512]{0,1:T(8,128)} async-done(((f32[1024,64]{0,1:T(8,128)}), f32[1024,512]{0,1:T(8,128)}) %all-gather.5.cloned.1.call-update) | async-done | bytes 2097168 | tf_op jit(solution)/shard_map/all_gather | solution.py:120
  304.6 5.0 %fusion.156 = f32[1024,128]{1,0:T(8,128)S(1)} fusion(f32[1024,512]{0,1:T(8,128)} %all-gather.5.cloned.1.call-done, f32[512,128]{1,0:T(8,128)S(1)} %copy-done.7), kind=kOutput, calls=%fused_computation.221 | convolution fusion | flops 805306368 | bytes 2883584 | tf_op jit(solution)/shard_map/dot_general | solution.py:28
  309.6 4.3 %fusion.21 = f32[1024,512]{0,1:T(8,128)} fusion(f32[128,512]{1,0:T(8,128)S(1)} %copy-done.10, f32[1024,128]{1,0:T(8,128)S(1)} %fusion.156), kind=kOutput, calls=%fused_computation.37 | convolution fusion | flops 813694976 | bytes 2883584 | tf_op jit(solution)/shard_map/dot_general | solution.py:28
  314.0 36.6 %reduce-scatter.2.cloned.1.call-done = f32[1024,64]{0,1:T(8,128)} async-done(((f32[1024,512]{0,1:T(8,128)}), f32[1024,64]{0,1:T(8,128)}) %reduce-scatter.2.cloned.1.call-update) | async-done | bytes 262160 | tf_op jit(solution)/shard_map/reduce_scatter | solution.py:123
  351.8 3.2 scatter_custom_fusion.1
  (94 shorter events, 18.6 us)
Async XLA Ops:
  6.5 17.9 %copy-start = (f32[1024,512]{1,0:T(8,128)S(1)}, f32[1024,512]{1,0:T(8,128)}, u32[]{:S(2)}) copy-start(f32[1024,512]{1,0:T(8,128)} %param.13) | copy-start | bytes 6291460
  12.1 27.0 %all-to-all-start = ((s32[32,1,3]{2,1,0:T(1,128)}), s32[32,1,3]{2,1,0:T(1,128)S(1)}, u32[]{:S(2)}, u32[]{:S(2)}) async-start(s32[32,1,3]{2,1,0:T(1,128)} %copy.52), calls=%async_computation | async-start | bytes 32768 | tf_op jit(solution)/shard_map/all_to_all | solution.py:99
  32.2 1.8 copy-start.5
  32.2 3.3 copy-start.6
  34.0 2.9 copy-start.2
  49.1 148.0 %all-to-all-start.1 = ((f32[32,3,128,128]{3,2,1,0:T(8,128)}), f32[32,3,128,128]{3,2,1,0:T(8,128)}, u32[]{:S(2)}, u32[]{:S(2)}) async-start(f32[32,3,128,128]{3,2,1,0:T(8,128)} %broadcast_select_fusion), calls=%async_computation.1 | async-start | bytes 12582912 | tf_op jit(solution)/shard_map/all_to_all | solution.py:101
  58.9 15.1 %copy-start.9 = (s32[8,6]{1,0:T(8,128)S(1)}, s32[8,6]{1,0:T(8,128)}, u32[]{:S(2)}) copy-start(s32[8,6]{1,0:T(8,128)} %param.17) | copy-start | bytes 580
  58.9 15.2 %copy-start.1 = (s32[256]{0:T(256)S(1)}, s32[256]{0:T(256)}, u32[]{:S(2)}) copy-start(s32[256]{0:T(256)} %param.15) | copy-start | bytes 3076
  58.9 200.9 %all-gather.3.cloned.1.call-start = ((), (), s32[]{:S(2)}) async-start(), calls=%async_computation.3 | async-start | bytes 2359296 | tf_op jit(solution)/shard_map/all_gather | solution.py:111
  61.3 23.9 %collective-permute-start.1 = (f32[2,128,128]{2,1,0:T(8,128)}, f32[2,128,128]{2,1,0:T(8,128)}, u32[]{:S(2)}, u32[]{:S(2)}) collective-permute-start(f32[2,128,128]{2,1,0:T(8,128)} %bitcast.1), channel_id=1, source_target_pairs={{8,0},{16,8},{24,16},{32,24},{40,32},{48,40},{56,48},{64,56},{72,6... | collective-permute-start | bytes 393224 | tf_op jit(solution)/shard_map/ppermute | solution.py:22
  64.3 20.9 %collective-permute-start = (f32[2,128,128]{2,1,0:T(8,128)}, f32[2,128,128]{2,1,0:T(8,128)}, u32[]{:S(2)}, u32[]{:S(2)}) collective-permute-start(f32[2,128,128]{2,1,0:T(8,128)} %bitcast), channel_id=1, source_target_pairs={{0,8},{8,16},{16,24},{24,32},{32,40},{40,48},{48,56},{56,64},{64,7... | collective-permute-start | bytes 393224 | tf_op jit(solution)/shard_map/ppermute | solution.py:21
  74.9 1.2 copy-start.11
  197.0 5.4 %copy-start.3 = (f32[8,1,128,128]{3,2,1,0:T(8,128)S(1)}, f32[8,1,128,128]{3,2,1,0:T(8,128)}, u32[]{:S(2)}) copy-start(f32[8,1,128,128]{3,2,1,0:T(8,128)} %fusion.23) | copy-start | bytes 1572868
  202.5 2.8 copy-start.4
  212.5 47.3 %copy-start.8 = (f32[512,64]{0,1:T(8,128)S(1)}, f32[512,64]{0,1:T(8,128)}, u32[]{:S(2)}) copy-start(f32[512,64]{0,1:T(8,128)} %param.23) | copy-start | bytes 393220
  223.0 81.6 %copy-start.7 = (f32[512,128]{1,0:T(8,128)S(1)}, f32[512,128]{1,0:T(8,128)}, u32[]{:S(2)}) copy-start(f32[512,128]{1,0:T(8,128)} %param.24) | copy-start | bytes 786436
  224.0 80.6 %all-gather.5.cloned.1.call-start = ((), (), s32[]{:S(2)}) async-start(), calls=%async_computation.4 | async-start | bytes 2359296 | tf_op jit(solution)/shard_map/all_gather | solution.py:120
  224.0 85.6 %copy-start.10 = (f32[128,512]{1,0:T(8,128)S(1)}, f32[128,512]{1,0:T(8,128)}, u32[]{:S(2)}) copy-start(f32[128,512]{1,0:T(8,128)} %param.25) | copy-start | bytes 786436
  277.9 72.7 %reduce-scatter.2.cloned.1.call-start = ((), (), s32[]{:S(2)}) async-start(), calls=%async_computation.5 | async-start | bytes 2359296 | tf_op jit(solution)/shard_map/reduce_scatter | solution.py:123
Sparse Core Ops, SparseCore 0:
  224.1 35.6 all-gather.2
  278.0 26.5 all-gather.4
  314.1 36.4 reduce-scatter.1
where the time goes:
time: 368 us; the launch traced here: 363 us
  waiting for transfers between devices  209 us (57%)
  matrix products  40.4 us (11%)
  local copies, waits for them, and re-layouts  36.7 us (10%)
  starting transfers between devices  28.1 us (8%)
  other arithmetic  20.9 us (6%)
  blocking collectives  14.2 us (4%)
  between operations  13.7 us (4%)
    all_to_all x1, waiting for transfers between devices, shards(): lax.all_to_all(blocks, 'dom', split_axis=0, concat_axis=0, tiled=True)  106 us
    reduce_scatter x1, waiting for transfers between devices, shards(): lax.psum_scatter(partials, 'head', scatter_dimension=1, tiled=True)  36.6 us
    all_gather x1, waiting for transfers between devices, shards(): lax.all_gather(heads_flat, 'head', axis=1, tiled=True)  35.8 us
    all_gather x1, waiting for transfers between devices, shards(): hidden = matmul(lax.all_gather(normed, 'head', axis=1, tiled=True), w_up)  26.5 us
    dot_general x8, matrix products, matmul(): jnp.dot(left, right, preferred_element_type=jnp.float32, precision=highest)  23.7 us
    psum x1, blocking collectives, shards(): lax.psum((jnp.sum(residual, 1), jnp.sum(residual * residual, 1)), 'head')  14.2 us
    all_to_all x1, starting transfers between devices, shards(): lax.all_to_all(request, 'dom', split_axis=0, concat_axis=0, tiled=True)  11.6 us
    dot_general x1, matrix products, partial_softmax(): jnp.einsum('bhqk,bkhd->bqhd', weights, value_rows, precision=highest)  10.5 us
  transfers between devices with their start and end apart: 7, of which 5 were waited for; matrix products, arithmetic and copies ran while one was open for 10% of the time, Pallas kernels for 0%

commit v1 on v0

--- a/solution.py
+++ b/solution.py
@@ -9,6 +9,28 @@
 NE = 6
 LW = 2
 highest = lax.Precision.HIGHEST
+
+
+def laid_out(blocks, dim):
+    lengths = list(blocks.shape[1:])
+    lengths[dim] *= blocks.shape[0]
+    return jnp.moveaxis(blocks, 0, dim).reshape(lengths)
+
+
+def collect(x, axis, dim):
+    size = lax.axis_size(axis)
+    pairs = [(i, (i + 1) % size) for i in range(size)]
+    back = [(b, a) for a, b in pairs]
+    lower, upper = ([], [])
+    for step in range(size - 1):
+        if step % 2 == 0:
+            lower.append(lax.ppermute(lower[-1] if lower else x, axis, pairs))
+        else:
+            upper.append(lax.ppermute(upper[-1] if upper else x, axis, back))
+    tiles = jnp.stack([*lower[::-1], x, *upper])
+    shift = lax.axis_index(axis) - len(lower)
+    tiles = tiles[(jnp.arange(size) - shift) % size]
+    return laid_out(tiles, dim)
 
 
 def with_halo(value, sides, width):
@@ -117,7 +139,7 @@
     row_mean = row_sums / D
     row_var = row_squares / D - row_mean * row_mean
     normed = (residual - row_mean[:, None]) * lax.rsqrt(row_var + 1e-05)[:, None]
-    hidden = matmul(lax.all_gather(normed, "head", axis=1, tiled=True), w_up)
+    hidden = matmul(collect(normed, "head", 1), w_up)
     activated = jax.nn.gelu(hidden, approximate=False)
     partials = matmul(activated, w_down)
     feed_forward = lax.psum_scatter(partials, "head", scatter_dimension=1, tiled=True)

time: 368 us -> 381 us (1.035)
  local copies, waits for them, and re-layouts: 36.7 us -> 47.4 us
  waiting for transfers between devices: 209 us -> 200 us
  starting transfers between devices: 28.1 us -> 36.7 us
    all_gather x1 -> x0, waiting for transfers between devices: 26.5 us -> none  [shards(): hidden = matmul(lax.all_gather(normed, 'head', axis=1, tiled=True), w_up)]
    ppermute x0 -> x7, waiting for transfers between devices: none -> 19.5 us  [the longest x4 19.5 us: collect(): lower.append(lax.ppermute(lower[-1] if lower else x, axis, pairs))]
    ppermute x0 -> x7, starting transfers between devices: none -> 8.9 us  [the longest x3 8.87 us: collect(): upper.append(lax.ppermute(upper[-1] if upper else x, axis, back))]
    unnamed x26 -> x34, local copies, waits for them, and re-layouts: 1.57 us -> 7.82 us
  transfers between devices with their start and end apart: 7 -> 13, of which waited for: 5 -> 8; matrix products, arithmetic and copies ran while one was open for 10% -> 12% of each run, Pallas kernels for 0% -> 0%
where the time goes in v1:
time: 381 us; the launch traced here: 375 us
  waiting for transfers between devices  200 us (52%)
  local copies, waits for them, and re-layouts  47.4 us (12%)
  matrix products  40.4 us (11%)
  starting transfers between devices  36.7 us (10%)
  other arithmetic  21.6 us (6%)
  blocking collectives  14.5 us (4%)
  between operations  14 us (4%)
    all_to_all x1, waiting for transfers between devices, shards(): lax.all_to_all(blocks, 'dom', split_axis=0, concat_axis=0, tiled=True)  106 us
    all_gather x1, waiting for transfers between devices, shards(): lax.all_gather(heads_flat, 'head', axis=1, tiled=True)  35.8 us
    reduce_scatter x1, waiting for transfers between devices, shards(): lax.psum_scatter(partials, 'head', scatter_dimension=1, tiled=True)  35.2 us
    dot_general x8, matrix products, matmul(): jnp.dot(left, right, preferred_element_type=jnp.float32, precision=highest)  23.8 us
    ppermute x4, waiting for transfers between devices, collect(): lower.append(lax.ppermute(lower[-1] if lower else x, axis, pairs))  19.5 us
    psum x1, blocking collectives, shards(): lax.psum((jnp.sum(residual, 1), jnp.sum(residual * residual, 1)), 'head')  14.5 us
    all_to_all x1, starting transfers between devices, shards(): lax.all_to_all(request, 'dom', split_axis=0, concat_axis=0, tiled=True)  11.6 us
    dot_general x1, matrix products, partial_softmax(): jnp.einsum('bhqk,bkhd->bqhd', weights, value_rows, precision=highest)  10.5 us
  transfers between devices with their start and end apart: 13, of which 8 were waited for; matrix products, arithmetic and copies ran while one was open for 12% of the time, Pallas kernels for 0%

profile of v1, /device:TPU:2, one launch (start us, length us, event | category | flops | bytes accessed | tf_op | source)
XLA Modules:
  0.0 374.9 jit_solution(15892633168308145555)
XLA Ops:
  8.6 2.8 scatter_fusion
  12.1 11.6 %all-to-all-start = ((s32[32,1,3]{2,1,0:T(1,128)}), s32[32,1,3]{2,1,0:T(1,128)S(1)}, u32[]{:S(2)}, u32[]{:S(2)}) async-start(s32[32,1,3]{2,1,0:T(1,128)} %copy.52), calls=%async_computation | async-start | bytes 32768 | tf_op jit(solution)/shard_map/all_to_all | solution.py:121
  25.1 4.9 %gather_fusion = f32[1024,512]{1,0:T(8,128)} fusion(f32[1024,512]{1,0:T(8,128)S(1)} %copy-done, s32[1024]{0:T(1024)S(1)} %broadcast_clamp_fusion), kind=kCustom, calls=%fused_computation | custom fusion | bytes 4198400 | tf_op jit(solution)/shard_map/jit(_take)/gather | solution.py:95
  30.0 2.9 copy.47
  40.2 3.6 gather_fusion.2
  43.9 5.9 %broadcast_select_fusion = f32[32,3,128,128]{3,2,1,0:T(8,128)} fusion(f32[32,3,128,128]{3,2,1,0:T(8,128)} %bitcast.103, pred[32,3]{1,0:T(8,128)(4,1)S(1)} %copy.54), kind=kLoop, calls=%fused_computation.18 | loop fusion | flops 1572864 | bytes 12583008 | tf_op jit(solution)/shard_map/jit(_take)/select_n | solution.py:120
  49.8 9.8 %all-to-all-start.1 = ((f32[32,3,128,128]{3,2,1,0:T(8,128)}), f32[32,3,128,128]{3,2,1,0:T(8,128)}, u32[]{:S(2)}, u32[]{:S(2)}) async-start(f32[32,3,128,128]{3,2,1,0:T(8,128)} %broadcast_select_fusion), calls=%async_computation.1 | async-start | bytes 12582912 | tf_op jit(solution)/shard_map/all_to_all | solution.py:123
  65.0 4.1 %collective-permute-start = (f32[2,128,128]{2,1,0:T(8,128)}, f32[2,128,128]{2,1,0:T(8,128)}, u32[]{:S(2)}, u32[]{:S(2)}) collective-permute-start(f32[2,128,128]{2,1,0:T(8,128)} %bitcast), channel_id=1, source_target_pairs={{0,8},{8,16},{16,24},{24,32},{32,40},{40,48},{48,56},{56,64},{64,7... | collective-permute-start | bytes 393224 | tf_op jit(solution)/shard_map/ppermute | solution.py:43
  69.1 2.4 fusion.157
  76.9 3.7 convolution_bitcast_fusion
  82.4 3.4 collective-permute-done.1
  88.7 2.7 broadcast_select_fusion.2
  91.4 106.3 %all-to-all-done.1 = f32[32,3,128,128]{3,2,1,0:T(8,128)} async-done(((f32[32,3,128,128]{3,2,1,0:T(8,128)}), f32[32,3,128,128]{3,2,1,0:T(8,128)}, u32[]{:S(2)}, u32[]{:S(2)}) %all-to-all-start.1) | async-done | bytes 6291488 | tf_op jit(solution)/shard_map/all_to_all | solution.py:123
  197.7 5.4 %gather_fusion.3 = f32[48,128,128]{2,1,0:T(8,128)} fusion(f32[32,3,128,128]{3,2,1,0:T(8,128)} %all-to-all-done.1, s32[48]{0:T(128)S(1)} %get-tuple-element.11), kind=kCustom, calls=%fused_computation.3 | custom fusion | bytes 6291840 | tf_op jit(solution)/shard_map/gather | solution.py:124
  203.1 2.8 pad_maximum_fusion
  205.9 6.1 %fusion.153 = (f32[8,128]{1,0:T(8,128)S(1)}, f32[8,128,1280]{2,1,0:T(8,128)S(1)}) fusion(f32[8,1280,128]{2,1,0:T(8,128)S(1)} %bitcast.101, f32[8,8,8,128]{3,2,1,0:T(8,128)S(1)} %copy-done.4, pred[8,1280]{1,0:T(8,128)(4,1)S(1)} %add_bitcast_fusion), kind=kOutput, calls=%fused_computation.232 | convolution fusion | flops 1010564096 | bytes 10762240 | tf_op jit(solution)/shard_map/bqhd,bkhd->bhqk/dot_general | solution.py:59
  213.2 10.5 %fusion.16 = f32[8,128,1,64]{1,3,0,2:T(8,128)S(1)} fusion(f32[8,128,1280]{2,1,0:T(8,128)S(1)} %get-tuple-element.22, f32[8,128]{1,0:T(8,128)S(1)} %get-tuple-element.21, pred[8,1280]{1,0:T(8,128)(4,1)S(1)} %add_bitcast_fusion, f32[8,1280,128]{2,1,0:T(8,128)S(1)} %bitcast.102, f32[8,128]{1,0:T(8,128)S(1)} %fusion.6), kind=kOutput, calls=%fused_computation.26 | convolution fusion | flops 1009319936 | bytes 10766336 | tf_op jit(solution)/shard_map/bhqk,bkhd->bqhd/dot_general | solution.py:66
  224.7 35.8 %all-gather.2.cloned.1.call-done = f32[1024,512]{0,1:T(8,128)} async-done(((f32[1024,64]{0,1:T(8,128)}), f32[1024,512]{0,1:T(8,128)}) %all-gather.2.cloned.1.call-update) | async-done | bytes 2097168 | tf_op jit(solution)/shard_map/all_gather | solution.py:133
  260.5 3.0 fusion.152
  263.5 14.5 %all-reduce = (f32[1024]{0:T(1024)S(1)}, f32[1024]{0:T(1024)S(1)}) all-reduce(f32[1024]{0:T(1024)S(1)} %get-tuple-element.6, f32[1024]{0:T(1024)S(1)} %get-tuple-element.5), channel_id=1, replica_groups=mesh['dom'=32,'head'=8] {'head'}, use_global_device_ids=true, to_apply=%region_8.9 | all-reduce | flops 2048 | bytes 16384 | tf_op jit(solution)/shard_map/psum | solution.py:136
  278.1 7.0 %collective-permute-done.2 = f32[1024,64]{0,1:T(8,128)S(1)} collective-permute-done((f32[1024,64]{0,1:T(8,128)S(1)}, f32[1024,64]{0,1:T(8,128)S(1)}, u32[]{:S(2)}, u32[]{:S(2)}) %collective-permute-start.2) | collective-permute-done | bytes 262176 | tf_op jit(solution)/shard_map/ppermute | solution.py:27
  285.1 3.0 collective-permute-start.6
  288.0 4.1 %collective-permute-done.3 = f32[1024,64]{0,1:T(8,128)S(1)} collective-permute-done((f32[1024,64]{0,1:T(8,128)S(1)}, f32[1024,64]{0,1:T(8,128)S(1)}, u32[]{:S(2)}, u32[]{:S(2)}) %collective-permute-start.3) | collective-permute-done | bytes 262176 | tf_op jit(solution)/shard_map/ppermute | solution.py:27
  292.1 3.0 collective-permute-start.7
  295.0 4.2 %collective-permute-done.4 = f32[1024,64]{0,1:T(8,128)} collective-permute-done((f32[1024,64]{0,1:T(8,128)S(1)}, f32[1024,64]{0,1:T(8,128)}, u32[]{:S(2)}, u32[]{:S(2)}) %collective-permute-start.4) | collective-permute-done | bytes 262176 | tf_op jit(solution)/shard_map/ppermute | solution.py:27
  299.2 3.0 collective-permute-start.8
  302.2 4.3 %collective-permute-done.5 = f32[1024,64]{0,1:T(8,128)} collective-permute-done((f32[1024,64]{0,1:T(8,128)}, f32[1024,64]{0,1:T(8,128)}, u32[]{:S(2)}, u32[]{:S(2)}) %collective-permute-start.5) | collective-permute-done | bytes 262176 | tf_op jit(solution)/shard_map/ppermute | solution.py:27
  314.3 3.6 gather_fusion.7
  317.9 5.1 %fusion.158 = f32[1024,128]{1,0:T(8,128)S(1)} fusion(f32[1024,512]{0,1:T(8,128)} %bitcast.104, f32[512,128]{1,0:T(8,128)S(1)} %copy-done.7), kind=kOutput, calls=%fused_computation.237 | convolution fusion | flops 805306368 | bytes 2883584 | tf_op jit(solution)/shard_map/dot_general | solution.py:50
  323.0 4.3 %fusion.21 = f32[1024,512]{0,1:T(8,128)} fusion(f32[128,512]{1,0:T(8,128)S(1)} %copy-done.11, f32[1024,128]{1,0:T(8,128)S(1)} %fusion.158), kind=kOutput, calls=%fused_computation.38 | convolution fusion | flops 813694976 | bytes 2883584 | tf_op jit(solution)/shard_map/dot_general | solution.py:50
  327.3 35.2 %reduce-scatter.2.cloned.1.call-done = f32[1024,64]{0,1:T(8,128)} async-done(((f32[1024,512]{0,1:T(8,128)}), f32[1024,64]{0,1:T(8,128)}) %reduce-scatter.2.cloned.1.call-update) | async-done | bytes 262160 | tf_op jit(solution)/shard_map/reduce_scatter | solution.py:145
  363.7 3.2 scatter_custom_fusion.1
  (116 shorter events, 38.8 us)
Async XLA Ops:
  6.5 18.5 %copy-start = (f32[1024,512]{1,0:T(8,128)S(1)}, f32[1024,512]{1,0:T(8,128)}, u32[]{:S(2)}) copy-start(f32[1024,512]{1,0:T(8,128)} %param.13) | copy-start | bytes 6291460
  12.1 27.7 %all-to-all-start = ((s32[32,1,3]{2,1,0:T(1,128)}), s32[32,1,3]{2,1,0:T(1,128)S(1)}, u32[]{:S(2)}, u32[]{:S(2)}) async-start(s32[32,1,3]{2,1,0:T(1,128)} %copy.52), calls=%async_computation | async-start | bytes 32768 | tf_op jit(solution)/shard_map/all_to_all | solution.py:121
  32.9 1.8 copy-start.5
  34.7 2.9 copy-start.2
  34.7 1.5 copy-start.6
  49.8 148.0 %all-to-all-start.1 = ((f32[32,3,128,128]{3,2,1,0:T(8,128)}), f32[32,3,128,128]{3,2,1,0:T(8,128)}, u32[]{:S(2)}, u32[]{:S(2)}) async-start(f32[32,3,128,128]{3,2,1,0:T(8,128)} %broadcast_select_fusion), calls=%async_computation.1 | async-start | bytes 12582912 | tf_op jit(solution)/shard_map/all_to_all | solution.py:123
  59.6 200.9 %all-gather.2.cloned.1.call-start = ((), (), s32[]{:S(2)}) async-start(), calls=%async_computation.3 | async-start | bytes 2359296 | tf_op jit(solution)/shard_map/all_gather | solution.py:133
  60.3 14.5 %copy-start.10 = (s32[8,6]{1,0:T(8,128)S(1)}, s32[8,6]{1,0:T(8,128)}, u32[]{:S(2)}) copy-start(s32[8,6]{1,0:T(8,128)} %param.17) | copy-start | bytes 580
  60.3 14.7 %copy-start.1 = (s32[256]{0:T(256)S(1)}, s32[256]{0:T(256)}, u32[]{:S(2)}) copy-start(s32[256]{0:T(256)} %param.15) | copy-start | bytes 3076
  62.0 23.8 %collective-permute-start.1 = (f32[2,128,128]{2,1,0:T(8,128)}, f32[2,128,128]{2,1,0:T(8,128)}, u32[]{:S(2)}, u32[]{:S(2)}) collective-permute-start(f32[2,128,128]{2,1,0:T(8,128)} %bitcast.1), channel_id=1, source_target_pairs={{8,0},{16,8},{24,16},{32,24},{40,32},{48,40},{56,48},{64,56},{72,6... | collective-permute-start | bytes 393224 | tf_op jit(solution)/shard_map/ppermute | solution.py:44
  65.0 20.9 %collective-permute-start = (f32[2,128,128]{2,1,0:T(8,128)}, f32[2,128,128]{2,1,0:T(8,128)}, u32[]{:S(2)}, u32[]{:S(2)}) collective-permute-start(f32[2,128,128]{2,1,0:T(8,128)} %bitcast), channel_id=1, source_target_pairs={{0,8},{8,16},{16,24},{24,32},{32,40},{40,48},{48,56},{56,64},{64,7... | collective-permute-start | bytes 393224 | tf_op jit(solution)/shard_map/ppermute | solution.py:43
  76.0 1.0 copy-start.8
  76.7 4.0 %copy-start.12 = (s32[8]{0:T(128)S(1)}, s32[8]{0:T(128)}, u32[]{:S(2)}) copy-start(s32[8]{0:T(128)} %param.18) | copy-start | bytes 100
  197.7 5.4 %copy-start.3 = (f32[8,1,128,128]{3,2,1,0:T(8,128)S(1)}, f32[8,1,128,128]{3,2,1,0:T(8,128)}, u32[]{:S(2)}) copy-start(f32[8,1,128,128]{3,2,1,0:T(8,128)} %fusion.23) | copy-start | bytes 1572868
  203.1 2.8 copy-start.4
  213.2 47.3 %copy-start.9 = (f32[512,64]{0,1:T(8,128)S(1)}, f32[512,64]{0,1:T(8,128)}, u32[]{:S(2)}) copy-start(f32[512,64]{0,1:T(8,128)} %param.23) | copy-start | bytes 393220
  224.7 137.9 %reduce-scatter.2.cloned.1.call-start = ((), (), s32[]{:S(2)}) async-start(), calls=%async_computation.4 | async-start | bytes 2359296 | tf_op jit(solution)/shard_map/reduce_scatter | solution.py:145
  278.0 7.0 %collective-permute-start.2 = (f32[1024,64]{0,1:T(8,128)S(1)}, f32[1024,64]{0,1:T(8,128)S(1)}, u32[]{:S(2)}, u32[]{:S(2)}) collective-permute-start(f32[1024,64]{0,1:T(8,128)S(1)} %subtract_multiply_fusion), channel_id=1, source_target_pairs={{0,1},{1,2},{2,3},{3,4},{4,5},{5,6},{6,7},{7,0},{8,9},{9,10},{10,1... | collective-permute-start | bytes 786440 | tf_op jit(solution)/shard_map/ppermute | solution.py:27
  285.1 7.0 %collective-permute-start.3 = (f32[1024,64]{0,1:T(8,128)S(1)}, f32[1024,64]{0,1:T(8,128)S(1)}, u32[]{:S(2)}, u32[]{:S(2)}) collective-permute-start(f32[1024,64]{0,1:T(8,128)S(1)} %collective-permute-done.2), channel_id=1, source_target_pairs={{0,1},{1,2},{2,3},{3,4},{4,5},{5,6},{6,7},{7,0},{8,9},{9,10},{10,1... | collective-permute-start | bytes 786440 | tf_op jit(solution)/shard_map/ppermute | solution.py:27
  285.1 7.0 %collective-permute-start.6 = (f32[1024,64]{0,1:T(8,128)S(1)}, f32[1024,64]{0,1:T(8,128)S(1)}, u32[]{:S(2)}, u32[]{:S(2)}) collective-permute-start(f32[1024,64]{0,1:T(8,128)S(1)} %subtract_multiply_fusion), channel_id=1, source_target_pairs={{1,0},{2,1},{3,2},{4,3},{5,4},{6,5},{7,6},{0,7},{9,8},{10,9},{11,1... | collective-permute-start | bytes 786440 | tf_op jit(solution)/shard_map/ppermute | solution.py:29
  292.1 7.1 %collective-permute-start.4 = (f32[1024,64]{0,1:T(8,128)S(1)}, f32[1024,64]{0,1:T(8,128)}, u32[]{:S(2)}, u32[]{:S(2)}) collective-permute-start(f32[1024,64]{0,1:T(8,128)S(1)} %collective-permute-done.3), channel_id=1, source_target_pairs={{0,1},{1,2},{2,3},{3,4},{4,5},{5,6},{6,7},{7,0},{8,9},{9,10},{10,1... | collective-permute-start | bytes 786440 | tf_op jit(solution)/shard_map/ppermute | solution.py:27
  292.1 7.1 %collective-permute-start.7 = (f32[1024,64]{0,1:T(8,128)S(1)}, f32[1024,64]{0,1:T(8,128)S(1)}, u32[]{:S(2)}, u32[]{:S(2)}) collective-permute-start(f32[1024,64]{0,1:T(8,128)S(1)} %collective-permute-done.6), channel_id=1, source_target_pairs={{1,0},{2,1},{3,2},{4,3},{5,4},{6,5},{7,6},{0,7},{9,8},{10,9},{11,1... | collective-permute-start | bytes 786440 | tf_op jit(solution)/shard_map/ppermute | solution.py:29
  299.2 7.3 %collective-permute-start.5 = (f32[1024,64]{0,1:T(8,128)}, f32[1024,64]{0,1:T(8,128)}, u32[]{:S(2)}, u32[]{:S(2)}) collective-permute-start(f32[1024,64]{0,1:T(8,128)} %collective-permute-done.4), channel_id=1, source_target_pairs={{0,1},{1,2},{2,3},{3,4},{4,5},{5,6},{6,7},{7,0},{8,9},{9,10},{10,1... | collective-permute-start | bytes 786440 | tf_op jit(solution)/shard_map/ppermute | solution.py:27
  299.2 14.3 %collective-permute-start.8 = (f32[1024,64]{0,1:T(8,128)S(1)}, f32[1024,64]{0,1:T(8,128)S(1)}, u32[]{:S(2)}, u32[]{:S(2)}) collective-permute-start(f32[1024,64]{0,1:T(8,128)S(1)} %collective-permute-done.7), channel_id=1, source_target_pairs={{1,0},{2,1},{3,2},{4,3},{5,4},{6,5},{7,6},{0,7},{9,8},{10,9},{11,1... | collective-permute-start | bytes 786440 | tf_op jit(solution)/shard_map/ppermute | solution.py:29
  314.3 3.6 copy-start.7
  317.9 5.1 %copy-start.11 = (f32[128,512]{1,0:T(8,128)S(1)}, f32[128,512]{1,0:T(8,128)}, u32[]{:S(2)}) copy-start(f32[128,512]{1,0:T(8,128)} %param.25) | copy-start | bytes 786436
Sparse Core Ops, SparseCore 0:
  224.8 35.6 all-gather.1
  327.4 35.0 reduce-scatter.1
